TPU v7x, 256 devices: a whole 4x4x8 slice. The times are simulated.
256 devices in a mesh: dp: 16 (over y_hi, x, core), expert: 16 (over y_lo, z).
Axes of the slice: x: 4, y: 4 (y_hi: 2, y_lo: 2; y = y_hi * 2 + y_lo), z: 8, core: 2. Of those that a mesh axis runs over, the one named last changes fastest.
Arguments:
- tokens: bfloat16 [32768, 3072], P(('dp', 'expert')), parts along dimension 0, may hold values from -6 to 6
- w_gate: bfloat16 [3072, 8192], P(None, 'expert'), may hold values from -0.109375 to 0.109375
- w_up: bfloat16 [3072, 8192], P(None, 'expert'), may hold values from -0.109375 to 0.109375
- w_down: bfloat16 [8192, 3072], P('expert'), may hold values from -0.0625 to 0.0625
- route_ids: int32 [32768, 2], P(('dp', 'expert')), parts along dimension 0, may hold values from 0 to 7, as said below
- route_prob: float32 [32768], P(('dp', 'expert')), parts along dimension 0, may hold values from 0.5 to 0.95
- slot_index: int32 [32768], P(('dp', 'expert')), parts along dimension 0, may hold values from 0 to 64, as said below
Outputs:
- mixed: bfloat16 [32768, 3072], P(('dp', 'expert')), parts along dimension 0
There are 16 independent parts, one for each index of `dp`. A program takes and returns all parts, laid end to end along the dimension named above; an argument that names none is the same for every part. Nothing has to cross between parts.
Inputs may be any that keep to these rules, and one draw needn't show every extreme that they name: `route_ids`: each row names two different experts. `slot_index`: a token of whose two experts one is expert 0 holds its rank, in row order, among the tokens of its device that name expert 0; every other token holds 64. At most 64 of one device's 128 tokens name expert 0, and some device has exactly 64; the router's capacity of 64 tokens for expert 0 is counted over each aligned pair of 256 tokens (blocks 2k and 2k + 1) and is always filled, so those two devices have exactly 64 such tokens together.
All inputs are finite; a program needn't handle non-finite values.
Results may differ from a plain program's by a relative error of at most 0.023.
Values may be sent and summed in bfloat16 or wider, within the bound.
No kernel may reach another device: no remote copies, remote signals or barrier semaphores. Data moves between devices by JAX's collectives and lax.ppermute only.
A program may use at most 128 MiB of HBM per device.

v0:
```python
import jax
import jax.numpy as jnp
from jax import lax
from jax.sharding import PartitionSpec as P


def shards(tokens, w_gate, w_up, w_down, route_ids, route_prob, slot_index):
    local_count = tokens.shape[0]
    capacity = local_count // 2
    share = jnp.where(
        route_ids[:, 0] == 0, route_prob, jnp.where(route_ids[:, 1] == 0, 1.0 - route_prob, 0.0)
    )
    share = jnp.where(slot_index < capacity, share, 0.0)
    picker = slot_index[None, :] == jnp.arange(capacity, dtype=jnp.int32)[:, None]
    picker_half = picker.astype(jnp.bfloat16)
    source = jnp.dot(picker_half, tokens, preferred_element_type=jnp.float32).astype(jnp.bfloat16)
    row_share = jnp.dot(picker.astype(jnp.float32), share, precision=lax.Precision.HIGHEST)
    block = lax.all_gather(source, "expert", axis=0, tiled=True)
    gate = jnp.dot(block, w_gate, preferred_element_type=jnp.float32)
    up = jnp.dot(block, w_up, preferred_element_type=jnp.float32)
    hidden = (jax.nn.silu(gate) * up).astype(jnp.bfloat16)
    partial_value = jnp.dot(hidden, w_down, preferred_element_type=jnp.float32).astype(jnp.bfloat16)
    partial_value = lax.optimization_barrier(partial_value)
    terms = partial_value.astype(jnp.float32)
    down = lax.psum_scatter(
        terms.astype(jnp.bfloat16), "expert", scatter_dimension=0, tiled=True
    ).astype(jnp.float32)
    scaled = (row_share[:, None] * down).astype(jnp.bfloat16)
    placed = jnp.einsum("cr,cd->rd", picker_half, scaled, preferred_element_type=jnp.float32)
    return placed.astype(jnp.bfloat16)


def solution(mesh):
    return jax.shard_map(
        shards,
        mesh=mesh,
        in_specs=(
            P(("dp", "expert"), None),
            P(None, "expert"),
            P(None, "expert"),
            P("expert", None),
            P(("dp", "expert"), None),
            P(("dp", "expert")),
            P(("dp", "expert")),
        ),
        out_specs=P(("dp", "expert"), None),
        check_vma=False,
    )
```

profile of v0, /device:TPU:4, one launch (start us, length us, event | category | flops | bytes accessed | tf_op | source)
XLA Modules:
  0.0 208.1 jit_solution(16924911761300009242)
XLA Ops:
  6.5 0.0 copy-start
  6.5 0.0 all-gather.2.cloned.1.call-start
  6.5 2.3 %convolution_convert_fusion.2 = bf16[64,3072]{1,0:T(8,128)(2,1)} fusion(bf16[128,3072]{1,0:T(8,128)(2,1)} %param.7, s32[128]{0:T(128)} %param.13), kind=kOutput, calls=%fused_computation.2 | convolution fusion | flops 50536448 | bytes 1180160 | tf_op jit(solution)/shard_map/dot_general | solution.py:16
  8.8 0.0 all-gather.2.cloned.1.call-update
  8.9 0.0 reduce-scatter.2.cloned.1.call-start
  8.9 85.4 %all-gather.2.cloned.1.call-done = bf16[1024,3072]{1,0:T(8,128)(2,1)} async-done(((bf16[64,3072]{1,0:T(8,128)(2,1)}), bf16[1024,3072]{1,0:T(8,128)(2,1)}) %all-gather.2.cloned.1.call-update) | async-done | bytes 6291472 | tf_op jit(solution)/shard_map/all_gather | solution.py:18
  94.3 8.5 %fusion.18 = f32[1024,512]{1,0:T(8,128)} fusion(bf16[1024,3072]{1,0:T(8,128)(2,1)} %all-gather.2.cloned.1.call-done, bf16[3072,512]{1,0:T(8,128)(2,1)} %param.8), kind=kOutput, calls=%fused_computation.27 | convolution fusion | flops 3221225472 | bytes 11534336 | tf_op jit(solution)/shard_map/dot_general | solution.py:19
  102.8 0.0 copy-done
  102.8 11.9 %convolution_convert_fusion = bf16[1024,3072]{1,0:T(8,128)(2,1)} fusion(bf16[512,3072]{1,0:T(8,128)(2,1)S(1)} %copy-done, f32[1024,512]{1,0:T(8,128)} %fusion.18, bf16[1024,3072]{1,0:T(8,128)(2,1)} %all-gather.2.cloned.1.call-done, bf16[3072,512]{1,0:T(8,128)(2,1)} %param.9), kind=kOutput, calls=%fused_computation | convolution fusion | flops 6448742400 | bytes 20971520 | tf_op jit(solution)/shard_map/dot_general | solution.py:22
  114.7 0.0 copy-start.1
  114.7 0.0 copy-start.2
  114.7 0.0 copy-start.3
  114.7 0.0 reduce-scatter.2.cloned.1.call-update
  114.7 0.6 copy-done.1
  115.4 0.0 copy-done.2
  115.4 0.0 copy-done.3
  115.4 0.1 convolution_bitcast_fusion
  115.5 83.4 %reduce-scatter.2.cloned.1.call-done = bf16[64,3072]{1,0:T(8,128)(2,1)} async-done(((bf16[1024,3072]{1,0:T(8,128)(2,1)}), bf16[64,3072]{1,0:T(8,128)(2,1)}) %reduce-scatter.2.cloned.1.call-update) | async-done | bytes 393232 | tf_op jit(solution)/shard_map/reduce_scatter | solution.py:25
  199.0 2.3 %convolution_convert_fusion.1 = bf16[128,3072]{1,0:T(8,128)(2,1)} fusion(bf16[64,3072]{1,0:T(8,128)(2,1)} %reduce-scatter.2.cloned.1.call-done, f32[64]{0:T(128)S(1)} %convolution_bitcast_fusion, s32[128]{0:T(128)S(1)} %copy-done.1), kind=kOutput, calls=%fused_computation.1 | convolution fusion | flops 51322880 | bytes 1180416 | tf_op jit(solution)/shard_map/cr,cd->rd/dot_general | solution.py:29
Async XLA Ops:
  6.5 96.2 %copy-start = (bf16[512,3072]{1,0:T(8,128)(2,1)S(1)}, bf16[512,3072]{1,0:T(8,128)(2,1)}, u32[]{:S(2)}) copy-start(bf16[512,3072]{1,0:T(8,128)(2,1)} %param.10) | copy-start | bytes 9437188
  6.5 87.8 %all-gather.2.cloned.1.call-start = ((), (), s32[]{:S(2)}) async-start(), calls=%async_computation.1 | async-start | bytes 6684672 | tf_op jit(solution)/shard_map/all_gather | solution.py:18
  8.9 190.1 %reduce-scatter.2.cloned.1.call-start = ((), (), s32[]{:S(2)}) async-start(), calls=%async_computation.2 | async-start | bytes 6684672 | tf_op jit(solution)/shard_map/reduce_scatter | solution.py:25
  114.7 0.7 copy-start.1
  114.7 0.7 copy-start.2
  114.7 0.7 copy-start.3
Sparse Core Ops, SparseCore 0:
  9.1 85.1 all-gather.1
  114.9 84.0 reduce-scatter.1
where the time goes:
time: 208 us
  waiting for transfers between devices  169 us (81%)
  matrix products  25.1 us (12%)
  between operations  13.4 us (6%)
    all_gather x1, waiting for transfers between devices, shards(): block = lax.all_gather(source, 'expert', axis=0, tiled=True)  85.4 us
    reduce_scatter x1, waiting for transfers between devices, shards(): lax.psum_scatter(terms.astype(jnp.bfloat16), 'expert', scatter_dimension=...  83.4 us
    dot_general x1, matrix products, shards(): jnp.dot(hidden, w_down, preferred_element_type=jnp.float32)  11.9 us
    dot_general x1, matrix products, shards(): gate = jnp.dot(block, w_gate, preferred_element_type=jnp.float32)  8.46 us
  transfers between devices with their start and end apart: 2, of which 2 were waited for; matrix products, arithmetic and copies ran while one was open for 0% of the time, Pallas kernels for 0%

commit v1 on v0

--- a/solution.py
+++ b/solution.py
@@ -2,6 +2,11 @@
 import jax.numpy as jnp
 from jax import lax
 from jax.sharding import PartitionSpec as P
+
+
+def swapped_in(array, mesh_axis, dim):
+    stack = jnp.stack([array] * lax.axis_size(mesh_axis))
+    return jnp.concatenate(lax.all_to_all(stack, mesh_axis, 0, 0), axis=dim)
 
 
 def shards(tokens, w_gate, w_up, w_down, route_ids, route_prob, slot_index):
@@ -15,7 +20,7 @@
     picker_half = picker.astype(jnp.bfloat16)
     source = jnp.dot(picker_half, tokens, preferred_element_type=jnp.float32).astype(jnp.bfloat16)
     row_share = jnp.dot(picker.astype(jnp.float32), share, precision=lax.Precision.HIGHEST)
-    block = lax.all_gather(source, "expert", axis=0, tiled=True)
+    block = swapped_in(source, "expert", 0)
     gate = jnp.dot(block, w_gate, preferred_element_type=jnp.float32)
     up = jnp.dot(block, w_up, preferred_element_type=jnp.float32)
     hidden = (jax.nn.silu(gate) * up).astype(jnp.bfloat16)

time: 208 us -> 272 us (1.31)
  blocking collectives: 0 us -> 149 us
  waiting for transfers between devices: 169 us -> 84.6 us
  matrix products: 25.1 us -> 20.6 us
  local copies, waits for them, and re-layouts: 0.67 us -> 4.1 us
    all_to_all x0 -> x1, blocking collectives: none -> 149 us  [swapped_in(): return jnp.concatenate(lax.all_to_all(stack, mesh_axis, 0, 0), axis=dim)]
    all_gather x1 -> x0, waiting for transfers between devices: 85.4 us -> none  [shards(): block = lax.all_gather(source, 'expert', axis=0, tiled=True)]
    dot_general x1, matrix products: 8.46 us -> 4.76 us  [shards(): gate = jnp.dot(block, w_gate, preferred_element_type=jnp.float32)]
  transfers between devices with their start and end apart: 2 -> 1, of which waited for: 2 -> 1; matrix products, arithmetic and copies ran while one was open for 0% -> 0% of each run, Pallas kernels for 0% -> 0%
where the time goes in v1:
time: 272 us
  blocking collectives  149 us (55%)
  waiting for transfers between devices  84.6 us (31%)
  matrix products  20.6 us (8%)
  between operations  13.4 us (5%)
  local copies, waits for them, and re-layouts  4.1 us (2%)
    all_to_all x1, blocking collectives, swapped_in(): return jnp.concatenate(lax.all_to_all(stack, mesh_axis, 0, 0), axis=dim)  149 us
    reduce_scatter x1, waiting for transfers between devices, shards(): lax.psum_scatter(terms.astype(jnp.bfloat16), 'expert', scatter_dimension=...  84.5 us
    dot_general x1, matrix products, shards(): jnp.dot(hidden, w_down, preferred_element_type=jnp.float32)  11.9 us
  transfers between devices with their start and end apart: 1, of which 1 were waited for; matrix products, arithmetic and copies ran while one was open for 0% of the time, Pallas kernels for 0%

profile of v1, /device:TPU:4, one launch (start us, length us, event | category | flops | bytes accessed | tf_op | source)
XLA Modules:
  0.0 271.7 jit_solution(11976089837104492171)
XLA Ops:
  6.5 0.0 copy-start
  6.5 0.0 reduce-scatter.2.cloned.1.call-start
  6.5 1.6 convolution_convert_fusion.2
  8.1 0.8 stack.2
  8.9 0.0 copy-start.3
  8.9 148.9 %all_to_all.5 = bf16[16,64,3072]{2,1,0:T(8,128)(2,1)S(1)} all-to-all(bf16[16,64,3072]{2,1,0:T(8,128)(2,1)S(1)} %stack.2), channel_id=1, replica_groups=mesh['dp'=16,'expert'=16] {'expert'}, dimensions={0} | all-to-all | bytes 12582912 | tf_op jit(solution)/shard_map/all_to_all | solution.py:9
  157.8 0.0 copy-start.1
  157.8 2.6 copy-done.1
  160.5 0.0 copy-done.3
  160.5 4.8 %fusion.18 = f32[1024,512]{1,0:T(8,128)} fusion(bf16[1024,3072]{1,0:T(8,128)(2,1)S(1)} %bitcast.22, bf16[3072,512]{1,0:T(8,128)(2,1)S(1)} %copy-done.3), kind=kOutput, calls=%fused_computation.27 | convolution fusion | flops 3221225472 | bytes 11534336 | tf_op jit(solution)/shard_map/dot_general | solution.py:24
  165.2 0.0 copy-done
  165.2 11.9 %convolution_convert_fusion = bf16[1024,3072]{1,0:T(8,128)(2,1)} fusion(bf16[512,3072]{1,0:T(8,128)(2,1)S(1)} %copy-done, f32[1024,512]{1,0:T(8,128)} %fusion.18, bf16[1024,3072]{1,0:T(8,128)(2,1)} %bitcast.23, bf16[3072,512]{1,0:T(8,128)(2,1)} %param.9), kind=kOutput, calls=%fused_computation | convolution fusion | flops 6448742400 | bytes 20971520 | tf_op jit(solution)/shard_map/dot_general | solution.py:27
  177.1 0.0 copy-start.2
  177.1 0.0 copy-start.4
  177.2 0.0 copy-start.5
  177.2 0.0 reduce-scatter.2.cloned.1.call-update
  177.2 0.6 copy-done.2
  177.8 0.0 copy-done.4
  177.8 0.0 copy-done.5
  177.8 0.1 convolution_bitcast_fusion
  178.0 84.5 %reduce-scatter.2.cloned.1.call-done = bf16[64,3072]{1,0:T(8,128)(2,1)} async-done(((bf16[1024,3072]{1,0:T(8,128)(2,1)}), bf16[64,3072]{1,0:T(8,128)(2,1)}) %reduce-scatter.2.cloned.1.call-update) | async-done | bytes 393232 | tf_op jit(solution)/shard_map/reduce_scatter | solution.py:30
  262.5 2.3 convolution_convert_fusion.1
Async XLA Ops:
  6.5 158.7 %copy-start = (bf16[512,3072]{1,0:T(8,128)(2,1)S(1)}, bf16[512,3072]{1,0:T(8,128)(2,1)}, u32[]{:S(2)}) copy-start(bf16[512,3072]{1,0:T(8,128)(2,1)} %param.10) | copy-start | bytes 9437188
  6.5 256.0 %reduce-scatter.2.cloned.1.call-start = ((), (), s32[]{:S(2)}) async-start(), calls=%async_computation.2 | async-start | bytes 6684672 | tf_op jit(solution)/shard_map/reduce_scatter | solution.py:30
  8.9 151.6 %copy-start.3 = (bf16[3072,512]{1,0:T(8,128)(2,1)S(1)}, bf16[3072,512]{1,0:T(8,128)(2,1)}, u32[]{:S(2)}) copy-start(bf16[3072,512]{1,0:T(8,128)(2,1)} %param.8) | copy-start | bytes 9437188
  157.8 2.6 copy-start.1
  177.1 0.7 copy-start.2
  177.1 0.7 copy-start.4
  177.2 0.7 copy-start.5
Sparse Core Ops, SparseCore 0:
  177.3 85.1 reduce-scatter.1
